TPU v7x, 32 devices: a whole 2x2x4 slice. The times are simulated.
32 devices in a mesh: gx: 4 (over y, x), gy: 2 (over core), gz: 4 (over z).
Axes of the slice: x: 2, y: 2, z: 4, core: 2. Of those that a mesh axis runs over, the one named last changes fastest.
Arguments:
- thermal_field: float32 [32, 32, 512], P('gz', 'gy', 'gx'), may hold values from -2 to 4
- forcing_per_step: float32 [32, 32, 512], P('gz', 'gy', 'gx'), may hold values from 0.1 to 4
- substance_label: int32 [32, 32, 512], P('gz', 'gy', 'gx'), may hold values from 0 to 7
- thermal_conductivities: float32 [8], replicated, may hold values from 0.5 to 4
- patch_group_label: int32 [4, 4, 16], P('gz', 'gy', 'gx'), may hold values from 0 to 63, as said below
- drain_power_density: float32 [64], replicated, may hold values from 0.2 to 2
Outputs:
- next_thermal_field: float32 [32, 32, 512], P('gz', 'gy', 'gx')
- forcing_with_drain: float32 [32, 32, 512], P('gz', 'gy', 'gx')
Inputs may be any that keep to these rules, and one draw needn't show every extreme that they name: `patch_group_label`: every cluster labels exactly four tiles.
All inputs are finite; a program needn't handle non-finite values.
Results may differ from a plain program's by a relative error of at most 0.0003.
Values sent between devices are 32-bit elements; how exact they have to be, the bound alone decides.
A program may use at most 64 MiB of HBM per device.

v0:
```python
import jax
import jax.numpy as jnp
from jax import lax
from jax.sharding import PartitionSpec as P

TX = 32
TY = 8


IMPLICIT_WEIGHT = 0.5
LATERAL_RATE = 100.0
VERTICAL_RATE = 400.0
SOURCE_STEP = 0.5
LEAK_SLOPE = 0.5


def padded(shard, sides, width):
    for axis, dim in sides:
        devices, length = (lax.axis_size(axis), shard.shape[dim])
        up = [(i, (i + 1) % devices) for i in range(devices - 1)]
        down = [(j, i) for i, j in up]
        last = lax.slice_in_dim(shard, length - width, length, axis=dim)
        first = lax.slice_in_dim(shard, 0, width, axis=dim)
        before = lax.ppermute(last, axis, up)
        after = lax.ppermute(first, axis, down)
        shard = jnp.concatenate([before, shard, after], axis=dim)
    return shard


def harmonic(first_k, second_k):
    return 2.0 * first_k * second_k / (first_k + second_k)


def chain_solve(gathered, position):
    zero_line = jnp.zeros_like(gathered[0, 0])

    def forward(state_pair, column):
        carry_const, carry_slope = state_pair
        divisor = 1.0 - carry_slope * column[2]
        offset = (column[0] - column[2] * carry_const) / divisor
        slope = -column[4] / divisor
        next_const = column[1] - column[3] * (carry_const - carry_slope * column[0]) / divisor
        next_slope = column[5] + column[3] * carry_slope * column[4] / divisor
        return ((next_const, next_slope), (carry_const, carry_slope, offset, slope))

    _, (consts, slopes, offsets, gradients) = lax.scan(forward, (zero_line, zero_line), gathered)

    def backward(next_value, item):
        offset, slope, carry_const, carry_slope = item
        value = offset + slope * next_value
        return (value, (next_value, carry_const - carry_slope * value))

    _, (right_values, left_values) = lax.scan(
        backward, zero_line, (offsets, gradients, consts, slopes), reverse=True
    )
    left_value = lax.dynamic_index_in_dim(left_values, position, 0, keepdims=False)
    right_value = lax.dynamic_index_in_dim(right_values, position, 0, keepdims=False)
    return (left_value, right_value)


def interface_x(coeffs):
    gathered = lax.all_gather(coeffs[None], "gx", axis=0, tiled=True)
    return chain_solve(gathered, lax.axis_index("gx"))


def interface_y(coeffs):
    gathered = lax.all_gather(coeffs[None], "gy", axis=0, tiled=True)
    return chain_solve(gathered, lax.axis_index("gy"))


def interface_z(coeffs):
    gathered = lax.all_gather(coeffs[None], "gz", axis=0, tiled=True)
    return chain_solve(gathered, lax.axis_index("gz"))


def shifted(values, offset, axis, filler):
    length = values.shape[axis]
    pad_shape = list(values.shape)
    pad_shape[axis] = abs(offset)
    padding = jnp.full(tuple(pad_shape), filler, values.dtype)
    if offset > 0:
        return jnp.concatenate(
            [padding, lax.slice_in_dim(values, 0, length - offset, axis=axis)], axis=axis
        )
    return jnp.concatenate(
        [lax.slice_in_dim(values, -offset, length, axis=axis), padding], axis=axis
    )


def reduce_lines(right_side, face, axis, interface):
    length = right_side.shape[axis]
    low_face = lax.slice_in_dim(face, 0, length, axis=axis)
    high_face = lax.slice_in_dim(face, 1, length + 1, axis=axis)
    places = lax.broadcasted_iota(jnp.int32, right_side.shape, axis)
    lower_band = -IMPLICIT_WEIGHT * low_face
    upper_band = -IMPLICIT_WEIGHT * high_face
    main_band = 1.0 + IMPLICIT_WEIGHT * (low_face + high_face)
    left_side = jnp.where(places == 0, lower_band, 0.0)
    right_edge = jnp.where(places == length - 1, upper_band, 0.0)
    sub_band = jnp.where(places == 0, 0.0, lower_band)
    super_band = jnp.where(places == length - 1, 0.0, upper_band)
    sources = [right_side, left_side, right_edge]
    stride = 1
    while stride < length:
        sub_down = shifted(sub_band, stride, axis, 0.0)
        main_down = shifted(main_band, stride, axis, 1.0)
        super_down = shifted(super_band, stride, axis, 0.0)
        sub_up = shifted(sub_band, -stride, axis, 0.0)
        main_up = shifted(main_band, -stride, axis, 1.0)
        super_up = shifted(super_band, -stride, axis, 0.0)
        factor_down = -sub_band / main_down
        factor_up = -super_band / main_up
        sources = [
            source
            + factor_down * shifted(source, stride, axis, 0.0)
            + factor_up * shifted(source, -stride, axis, 0.0)
            for source in sources
        ]
        main_band = main_band + factor_down * super_down + factor_up * sub_up
        sub_band = factor_down * sub_down
        super_band = factor_up * super_up
        stride = stride * 2
    local_part, left_part, right_part = [source / main_band for source in sources]
    coeffs = jnp.stack(
        [
            lax.index_in_dim(local_part, 0, axis, keepdims=False),
            lax.index_in_dim(local_part, length - 1, axis, keepdims=False),
            lax.index_in_dim(left_part, 0, axis, keepdims=False),
            lax.index_in_dim(left_part, length - 1, axis, keepdims=False),
            lax.index_in_dim(right_part, 0, axis, keepdims=False),
            lax.index_in_dim(right_part, length - 1, axis, keepdims=False),
        ]
    )
    left_value, right_value = interface(coeffs)
    return (
        local_part
        - jnp.expand_dims(left_value, axis) * left_part
        - jnp.expand_dims(right_value, axis) * right_part
    )


def per_device(
    thermal_field,
    forcing_per_step,
    substance_label,
    thermal_conductivities,
    patch_group_label,
    drain_power_density,
):
    layer_voxel_number, height_voxel_number, width_voxel_number = thermal_field.shape
    voxel_thermal_link = jnp.zeros(thermal_field.shape, jnp.float32)
    for level in range(thermal_conductivities.shape[0]):
        voxel_thermal_link = voxel_thermal_link + jnp.where(
            substance_label == level, thermal_conductivities[level], 0.0
        )
    joined_outputs = jnp.stack([thermal_field, voxel_thermal_link])
    bordered_array = padded(joined_outputs, (("gx", 3), ("gy", 2), ("gz", 1)), 1)
    bordered_thermal_field = bordered_array[0]
    padk = bordered_array[1]
    sideways_link_xaxis = LATERAL_RATE * harmonic(padk[1:-1, 1:-1, :-1], padk[1:-1, 1:-1, 1:])
    sideways_link_yaxis = LATERAL_RATE * harmonic(padk[1:-1, :-1, 1:-1], padk[1:-1, 1:, 1:-1])
    upward_link_strength = VERTICAL_RATE * harmonic(padk[:-1, 1:-1, 1:-1], padk[1:, 1:-1, 1:-1])
    energy_current = sideways_link_xaxis[:, :, 1:] * (
        bordered_thermal_field[1:-1, 1:-1, 2:] - thermal_field
    ) - sideways_link_xaxis[:, :, :-1] * (thermal_field - bordered_thermal_field[1:-1, 1:-1, :-2])
    energy_current = (
        energy_current
        + sideways_link_yaxis[:, 1:, :] * (bordered_thermal_field[1:-1, 2:, 1:-1] - thermal_field)
        - sideways_link_yaxis[:, :-1, :] * (thermal_field - bordered_thermal_field[1:-1, :-2, 1:-1])
    )
    energy_current = (
        energy_current
        + upward_link_strength[1:] * (bordered_thermal_field[2:, 1:-1, 1:-1] - thermal_field)
        - upward_link_strength[:-1] * (thermal_field - bordered_thermal_field[:-2, 1:-1, 1:-1])
    )
    residual = SOURCE_STEP * forcing_per_step + energy_current
    step_x = reduce_lines(residual, sideways_link_xaxis, 2, interface_x)
    step_y = reduce_lines(step_x, sideways_link_yaxis, 1, interface_y)
    upward_correction = reduce_lines(step_y, upward_link_strength, 0, interface_z)
    next_thermal_field = thermal_field + upward_correction
    patch_extents = (
        layer_voxel_number,
        height_voxel_number // TY,
        TY,
        width_voxel_number // TX,
        TX,
    )
    patch_power_sum = next_thermal_field.reshape(patch_extents).sum(axis=(0, 2, 4)).reshape(-1)
    local_labels = patch_group_label.reshape(-1)
    cluster_count = drain_power_density.shape[0]
    onehot = (local_labels[:, None] == jnp.arange(cluster_count)[None, :]).astype(jnp.float32)
    partial_value = jnp.dot(patch_power_sum, onehot, precision=lax.Precision.HIGHEST)
    cluster_cells = 4 * layer_voxel_number * TY * TX
    cluster_total = lax.psum(partial_value, ("gx", "gy", "gz"))
    leak_power = drain_power_density * jnp.exp(LEAK_SLOPE * (cluster_total / cluster_cells))
    tile_power = jnp.dot(onehot, leak_power, precision=lax.Precision.HIGHEST)
    forcing_with_drain = forcing_per_step.reshape(patch_extents) + tile_power.reshape(
        1, height_voxel_number // TY, 1, width_voxel_number // TX, 1
    )
    return (next_thermal_field, forcing_with_drain.reshape(forcing_per_step.shape))


def solution(mesh):
    in_specs = (
        P("gz", "gy", "gx"),
        P("gz", "gy", "gx"),
        P("gz", "gy", "gx"),
        P(),
        P("gz", "gy", "gx"),
        P(),
    )
    out_specs = (P("gz", "gy", "gx"), P("gz", "gy", "gx"))
    return jax.shard_map(
        per_device, mesh=mesh, in_specs=in_specs, out_specs=out_specs, check_vma=False
    )
```

profile of v0, /device:TPU:0, one launch (start us, length us, event | category | flops | bytes accessed | tf_op | source)
XLA Modules:
  0.0 110.0 jit_solution(4359483157431193662)
XLA Ops:
  0.6 1.6 %fusion.115 = (f32[1]{0:T(128)}, f32[1]{0:T(128)}, f32[1]{0:T(128)}, f32[1]{0:T(128)}, f32[1]{0:T(128)}, /*index=5*/f32[1]{0:T(128)}, f32[1]{0:T(128)}, f32[1]{0:T(128)}) fusion(f32[8]{0:T(128)} %param.21), kind=kLoop, calls=%fused_computation.347 | loop fusion | bytes 64 | tf_op jit(solution)/shard_map/slice | solution.py:154
  2.3 5.9 %add_bitcast_fusion = f32[1,8,16,128]{3,2,1,0:T(8,128)S(1)} fusion(s32[8,16,128]{2,1,0:T(8,128)} %param.20, f32[]{:T(128)} %bitcast.8, f32[]{:T(128)} %bitcast.7, f32[]{:T(128)} %bitcast.6, f32[]{:T(128)} %bitcast.5, f32[]{:T(128)} %bitcast.4, f32[]{:T(128)} %bitcast.3, f32[]{:T(128)} %bitcast.2, f32[]{:T(128)} %bitcast.1), kind=kLoop, calls=%fused_computation.203 | loop fusion | flops 376832 | bytes 131104 | tf_op jit(solution)/shard_map/stack | solution.py:156
  8.2 0.1 slice_maximum_fusion
  8.3 4.8 %collective-permute-start = (f32[2,8,16,1]{3,2,1,0:T(8,128)S(1)}, f32[2,8,16,1]{3,2,1,0:T(8,128)S(1)}, u32[]{:S(2)}, u32[]{:S(2)}) collective-permute-start(f32[2,8,16,1]{3,2,1,0:T(8,128)S(1)} %get-tuple-element.1143), channel_id=1, source_target_pairs={{0,8},{8,16},{16,24},{1,9},{9,17},{17,25},{2,10},{10,18},{18,26},{... | collective-permute-start | bytes 3080 | tf_op jit(solution)/shard_map/ppermute | solution.py:24
  13.2 1.3 %collective-permute-start.1 = (f32[2,8,16,1]{3,2,1,0:T(8,128)S(1)}, f32[2,8,16,1]{3,2,1,0:T(8,128)S(1)}, u32[]{:S(2)}, u32[]{:S(2)}) collective-permute-start(f32[2,8,16,1]{3,2,1,0:T(8,128)S(1)} %get-tuple-element.1144), channel_id=1, source_target_pairs={{8,0},{16,8},{24,16},{9,1},{17,9},{25,17},{10,2},{18,10},{26,18},{... | collective-permute-start | bytes 3080 | tf_op jit(solution)/shard_map/ppermute | solution.py:25
  14.5 1.4 %collective-permute-done = f32[2,8,16,1]{3,2,1,0:T(8,128)S(1)} collective-permute-done((f32[2,8,16,1]{3,2,1,0:T(8,128)S(1)}, f32[2,8,16,1]{3,2,1,0:T(8,128)S(1)}, u32[]{:S(2)}, u32[]{:S(2)}) %collective-permute-start) | collective-permute-done | bytes 1056 | tf_op jit(solution)/shard_map/ppermute | solution.py:24
  15.9 4.8 %collective-permute-done.1 = f32[2,8,16,1]{3,2,1,0:T(8,128)S(1)} collective-permute-done((f32[2,8,16,1]{3,2,1,0:T(8,128)S(1)}, f32[2,8,16,1]{3,2,1,0:T(8,128)S(1)}, u32[]{:S(2)}, u32[]{:S(2)}) %collective-permute-start.1) | collective-permute-done | bytes 1056 | tf_op jit(solution)/shard_map/ppermute | solution.py:25
  20.7 0.2 pad_maximum_fusion.11
  20.8 1.3 %collective-permute-start.2 = (f32[2,8,1,130]{3,1,2,0:T(8,128)S(1)}, f32[2,8,1,130]{3,1,2,0:T(8,128)S(1)}, u32[]{:S(2)}, u32[]{:S(2)}) collective-permute-start(f32[2,8,1,130]{3,1,2,0:T(8,128)S(1)} %copy.710), channel_id=1, source_target_pairs={{0,4},{1,5},{2,6},{3,7},{8,12},{9,13},{10,14},{11,15},{16,20},{17,... | collective-permute-start | bytes 24968 | tf_op jit(solution)/shard_map/ppermute | solution.py:24
  22.2 1.3 %collective-permute-start.3 = (f32[2,8,1,130]{3,1,2,0:T(8,128)S(1)}, f32[2,8,1,130]{3,1,2,0:T(8,128)S(1)}, u32[]{:S(2)}, u32[]{:S(2)}) collective-permute-start(f32[2,8,1,130]{3,1,2,0:T(8,128)S(1)} %copy.711), channel_id=1, source_target_pairs={{4,0},{5,1},{6,2},{7,3},{12,8},{13,9},{14,10},{15,11},{20,16},{21,... | collective-permute-start | bytes 24968 | tf_op jit(solution)/shard_map/ppermute | solution.py:25
  23.5 1.7 %collective-permute-done.3 = f32[2,8,1,130]{3,1,2,0:T(8,128)S(1)} collective-permute-done((f32[2,8,1,130]{3,1,2,0:T(8,128)S(1)}, f32[2,8,1,130]{3,1,2,0:T(8,128)S(1)}, u32[]{:S(2)}, u32[]{:S(2)}) %collective-permute-start.3) | collective-permute-done | bytes 8352 | tf_op jit(solution)/shard_map/ppermute | solution.py:25
  25.3 0.1 pad_maximum_fusion.7
  25.4 3.5 %collective-permute-start.4 = (f32[2,1,18,130]{3,2,1,0:T(8,128)S(1)}, f32[2,1,18,130]{3,2,1,0:T(8,128)S(1)}, u32[]{:S(2)}, u32[]{:S(2)}) collective-permute-start(f32[2,1,18,130]{3,2,1,0:T(8,128)S(1)} %get-tuple-element.1066), channel_id=1, source_target_pairs={{0,1},{1,2},{2,3},{4,5},{5,6},{6,7},{8,9},{9,10},{10,11},{12,13},{... | collective-permute-start | bytes 56168 | tf_op jit(solution)/shard_map/ppermute | solution.py:24
  28.9 1.3 %collective-permute-start.5 = (f32[2,1,18,130]{3,2,1,0:T(8,128)S(1)}, f32[2,1,18,130]{3,2,1,0:T(8,128)S(1)}, u32[]{:S(2)}, u32[]{:S(2)}) collective-permute-start(f32[2,1,18,130]{3,2,1,0:T(8,128)S(1)} %get-tuple-element.1067), channel_id=1, source_target_pairs={{1,0},{2,1},{3,2},{5,4},{6,5},{7,6},{9,8},{10,9},{11,10},{13,12},{... | collective-permute-start | bytes 56168 | tf_op jit(solution)/shard_map/ppermute | solution.py:25
  30.3 0.7 copy-done.2
  31.0 3.8 %collective-permute-done.5 = f32[2,1,18,130]{3,2,1,0:T(8,128)S(1)} collective-permute-done((f32[2,1,18,130]{3,2,1,0:T(8,128)S(1)}, f32[2,1,18,130]{3,2,1,0:T(8,128)S(1)}, u32[]{:S(2)}, u32[]{:S(2)}) %collective-permute-start.5) | collective-permute-done | bytes 18752 | tf_op jit(solution)/shard_map/ppermute | solution.py:25
  34.8 0.2 pad_maximum_fusion
  35.1 0.1 divide_multiply_fusion.1
  35.2 0.1 divide_multiply_fusion
  35.4 0.1 divide_multiply_fusion.2
  35.6 0.1 multiply_add_fusion.15
  35.8 0.8 copy-done.1
  36.6 0.2 fusion.14
  36.9 0.1 fusion.53
  37.0 0.1 multiply_add_fusion.35
  37.3 0.1 multiply_add_fusion.47
  37.5 0.1 fusion.83
  37.6 0.2 multiply_add_fusion.48
  38.0 0.1 multiply_add_fusion.45
  38.2 0.1 fusion.62
  38.3 0.1 fusion.79
  38.4 0.2 multiply_add_fusion.46
  38.8 0.1 multiply_add_fusion.43
  39.0 0.1 fusion.61
  39.2 0.2 multiply_add_fusion.44
  39.5 0.1 multiply_add_fusion.41
  40.0 0.2 multiply_add_fusion.42
  40.3 0.1 multiply_add_fusion.39
  40.8 0.2 multiply_add_fusion.40
  41.3 0.1 multiply_add_fusion.38
  41.7 0.1 add_divide_fusion.8
  41.8 0.2 slice_reduce_fusion.4
  42.2 0.2 add_divide_fusion.7
  42.3 0.2 slice_reduce_fusion.2
  42.5 0.2 slice_reduce_fusion
  42.7 8.6 %all-gather = f32[24,8,16]{2,1,0:T(8,128)S(1)} all-gather(f32[6,8,16]{2,1,0:T(8,128)S(1)} %constant_dynamic-update-slice_fusion), channel_id=2, replica_groups=mesh['gx'=4,'gy'=2,'gz'=4] {'gx'}, dimensions={0}, use_global_device_ids=true | all-gather | bytes 15360 | tf_op jit(solution)/shard_map/all_gather | solution.py:62
  51.4 0.3 while.120
  51.7 0.1 while.121
  51.9 0.1 multiply_subtract_fusion.4
  52.1 0.1 multiply_add_fusion.22
  52.3 0.1 multiply_add_fusion.20
  52.9 1.8 %all-gather.1 = f32[12,8,128]{2,1,0:T(8,128)S(1)} all-gather(f32[6,8,128]{2,1,0:T(8,128)S(1)} %constant_dynamic-update-slice_fusion.6), channel_id=3, replica_groups=mesh['gx'=4,'gy'=2,'gz'=4] {'gy'}, dimensions={0}, use_global_device_ids=true | all-gather | bytes 73728 | tf_op jit(solution)/shard_map/all_gather | solution.py:67
  54.8 0.1 while.122
  55.2 0.1 multiply_add_fusion.3
  55.9 13.8 %all-gather.2 = f32[24,16,128]{2,1,0:T(8,128)S(1)} all-gather(f32[6,16,128]{2,1,0:T(8,128)S(1)} %constant_dynamic-update-slice_fusion.12), channel_id=4, replica_groups=mesh['gx'=4,'gy'=2,'gz'=4] {'gz'}, dimensions={0}, use_global_device_ids=true | all-gather | bytes 245760 | tf_op jit(solution)/shard_map/all_gather | solution.py:72
  69.7 0.3 while.124
  70.1 0.1 while.125
  70.3 0.7 fusion.33
  71.0 0.1 reduce_sum.18
  71.2 0.2 convolution_bitcast_fusion.1
  71.4 37.5 %psum.7 = f32[64]{0:T(128)S(1)} all-reduce(f32[64]{0:T(128)S(1)} %convolution_bitcast_fusion.1), channel_id=1, replica_groups=mesh['gx'=4,'gy'=2,'gz'=4] {'gx','gy','gz'}, use_global_device_ids=true, to_apply=%region_14.15 | all-reduce | flops 64 | bytes 512 | tf_op jit(solution)/shard_map/psum | solution.py:194
  108.9 0.2 convolution_bitcast_fusion
  109.2 0.1 add.982
  109.3 0.6 broadcast_add_fusion
  (197 shorter events, 5.3 us)
Async XLA Ops:
  2.3 5.9 %copy-start = (f32[8,16,128]{2,1,0:T(8,128)S(1)}, f32[8,16,128]{2,1,0:T(8,128)}, u32[]{:S(2)}) copy-start(f32[8,16,128]{2,1,0:T(8,128)} %param.18) | copy-start | bytes 196612
  8.3 7.6 %collective-permute-start = (f32[2,8,16,1]{3,2,1,0:T(8,128)S(1)}, f32[2,8,16,1]{3,2,1,0:T(8,128)S(1)}, u32[]{:S(2)}, u32[]{:S(2)}) collective-permute-start(f32[2,8,16,1]{3,2,1,0:T(8,128)S(1)} %get-tuple-element.1143), channel_id=1, source_target_pairs={{0,8},{8,16},{16,24},{1,9},{9,17},{17,25},{2,10},{10,18},{18,26},{... | collective-permute-start | bytes 3080 | tf_op jit(solution)/shard_map/ppermute | solution.py:24
  13.2 7.5 %collective-permute-start.1 = (f32[2,8,16,1]{3,2,1,0:T(8,128)S(1)}, f32[2,8,16,1]{3,2,1,0:T(8,128)S(1)}, u32[]{:S(2)}, u32[]{:S(2)}) collective-permute-start(f32[2,8,16,1]{3,2,1,0:T(8,128)S(1)} %get-tuple-element.1144), channel_id=1, source_target_pairs={{8,0},{16,8},{24,16},{9,1},{17,9},{25,17},{10,2},{18,10},{26,18},{... | collective-permute-start | bytes 3080 | tf_op jit(solution)/shard_map/ppermute | solution.py:25
  20.8 2.6 %collective-permute-start.2 = (f32[2,8,1,130]{3,1,2,0:T(8,128)S(1)}, f32[2,8,1,130]{3,1,2,0:T(8,128)S(1)}, u32[]{:S(2)}, u32[]{:S(2)}) collective-permute-start(f32[2,8,1,130]{3,1,2,0:T(8,128)S(1)} %copy.710), channel_id=1, source_target_pairs={{0,4},{1,5},{2,6},{3,7},{8,12},{9,13},{10,14},{11,15},{16,20},{17,... | collective-permute-start | bytes 24968 | tf_op jit(solution)/shard_map/ppermute | solution.py:24
  22.2 3.1 %collective-permute-start.3 = (f32[2,8,1,130]{3,1,2,0:T(8,128)S(1)}, f32[2,8,1,130]{3,1,2,0:T(8,128)S(1)}, u32[]{:S(2)}, u32[]{:S(2)}) collective-permute-start(f32[2,8,1,130]{3,1,2,0:T(8,128)S(1)} %copy.711), channel_id=1, source_target_pairs={{4,0},{5,1},{6,2},{7,3},{12,8},{13,9},{14,10},{15,11},{20,16},{21,... | collective-permute-start | bytes 24968 | tf_op jit(solution)/shard_map/ppermute | solution.py:25
  25.4 5.7 %collective-permute-start.4 = (f32[2,1,18,130]{3,2,1,0:T(8,128)S(1)}, f32[2,1,18,130]{3,2,1,0:T(8,128)S(1)}, u32[]{:S(2)}, u32[]{:S(2)}) collective-permute-start(f32[2,1,18,130]{3,2,1,0:T(8,128)S(1)} %get-tuple-element.1066), channel_id=1, source_target_pairs={{0,1},{1,2},{2,3},{4,5},{5,6},{6,7},{8,9},{9,10},{10,11},{12,13},{... | collective-permute-start | bytes 56168 | tf_op jit(solution)/shard_map/ppermute | solution.py:24
  28.9 6.0 %collective-permute-start.5 = (f32[2,1,18,130]{3,2,1,0:T(8,128)S(1)}, f32[2,1,18,130]{3,2,1,0:T(8,128)S(1)}, u32[]{:S(2)}, u32[]{:S(2)}) collective-permute-start(f32[2,1,18,130]{3,2,1,0:T(8,128)S(1)} %get-tuple-element.1067), channel_id=1, source_target_pairs={{1,0},{2,1},{3,2},{5,4},{6,5},{7,6},{9,8},{10,9},{11,10},{13,12},{... | collective-permute-start | bytes 56168 | tf_op jit(solution)/shard_map/ppermute | solution.py:25
  30.3 0.7 copy-start.2
  35.8 0.8 copy-start.1
  71.4 37.5 %copy-start.3 = (f32[64]{0:T(128)S(1)}, f32[64]{0:T(128)}, u32[]{:S(2)}) copy-start(f32[64]{0:T(128)} %param.23) | copy-start | bytes 772
where the time goes:
time: 111 us; the launch traced here: 110 us
  blocking collectives  61.8 us (56%)
  starting transfers between devices  13.5 us (12%)
  other arithmetic  12.2 us (11%)
  waiting for transfers between devices  11.7 us (11%)
  local copies, waits for them, and re-layouts  8.1 us (7%)
  between operations  1.81 us (2%)
    psum x1, blocking collectives, per_device(): cluster_total = lax.psum(partial_value, ('gx', 'gy', 'gz'))  37.5 us
    all_gather x1, blocking collectives, interface_z(): gathered = lax.all_gather(coeffs[None], 'gz', axis=0, tiled=True)  13.8 us
    ppermute x3, waiting for transfers between devices, padded(): after = lax.ppermute(first, axis, down)  10.3 us
    ppermute x3, starting transfers between devices, padded(): before = lax.ppermute(last, axis, up)  9.62 us
    all_gather x1, blocking collectives, interface_x(): gathered = lax.all_gather(coeffs[None], 'gx', axis=0, tiled=True)  8.61 us
    another operation x2, other arithmetic, per_device(): joined_outputs = jnp.stack([thermal_field, voxel_thermal_link])  6.03 us
    ppermute x3, starting transfers between devices, padded(): after = lax.ppermute(first, axis, down)  3.88 us
    slice x50, local copies, waits for them, and re-layouts, shifted(): lax.slice_in_dim(values, 0, length - offset, axis=axis)  2.41 us
  transfers between devices with their start and end apart: 6, of which 4 were waited for; matrix products, arithmetic and copies ran while one was open for 0% of the time, Pallas kernels for 0%

commit v1 on v0

v1 whole, which is shorter than its diff:
```python
import functools

import jax
import jax.numpy as jnp
from jax import lax
from jax.experimental import pallas as pl
from jax.experimental.pallas import tpu as pltpu
from jax.sharding import PartitionSpec as P

TX = 32
TY = 8
LATERAL_RATE = 100.0
VERTICAL_RATE = 400.0
LEAK_SLOPE = 0.5
AXES = ("gx", "gy", "gz")
MESH = pl.DeviceIdType.MESH


def down(v, s):
    n = v.shape[0]
    s = s % n
    if s == 0:
        return v
    if v.ndim == 2 and s % 8:
        return pltpu.roll(v, s, 0)
    return jnp.concatenate([v[n - s:], v[: n - s]], axis=0)


def up(v, s):
    return down(v, v.shape[0] - s % v.shape[0])


def half_face(k, rate):
    below = down(k, 1)
    face = rate * k * below / (k + below)
    return jnp.where(lax.broadcasted_iota(jnp.int32, k.shape, 0) == 0, 0.0, face)


def factor(a):
    n = a.shape[0]
    rows = lax.broadcasted_iota(jnp.int32, a.shape, 0)
    first = jnp.where(rows == 0, 1.0, 0.0)
    last = jnp.where(rows == n - 1, 1.0, 0.0)
    excess = jnp.ones_like(a)
    b = up(a, 1)
    stages = []
    s = 1
    while s < n:
        inv = 1.0 / (excess + a + b)
        fd = a * down(inv, s)
        fu = b * up(inv, s)
        stages.append((s, fd, fu))
        excess = excess + fd * down(excess, s) + fu * up(excess, s)
        first = first + fd * down(first, s) + fu * up(first, s)
        last = last + fd * down(last, s) + fu * up(last, s)
        a = fd * down(a, s)
        b = up(a, 2 * s)
        s *= 2
    inv = 1.0 / excess
    return stages, inv, first * inv, last * inv


def apply_stages(stages, inv, r):
    for s, fd, fu in stages:
        r = r + fd * down(r, s) + fu * up(r, s)
    return r * inv


def chain_factor(mats):
    out = []
    slope = None
    for i in range(len(mats) - 1):
        den = mats[i][0] + mats[i + 1][1]
        if slope is not None:
            den = den - mats[i][2] * slope
        inv = 1.0 / den
        slope = mats[i + 1][2] * inv
        out.append((inv, slope, mats[i][2]))
    return out


def chain_flux(elim, firsts, lasts):
    ys = []
    for i, (inv, _, cross) in enumerate(elim):
        rhs = lasts[i] - firsts[i + 1]
        if i:
            rhs = rhs + cross * ys[-1]
        ys.append(rhs * inv)
    qs = [None] * len(ys)
    for i in reversed(range(len(ys))):
        qs[i] = ys[i] if i == len(ys) - 1 else ys[i] + elim[i][1] * qs[i + 1]
    return qs


def pick(values, index):
    out = jnp.zeros_like(values[0])
    for i, value in enumerate(values):
        out = jnp.where(index == i, value, out)
    return out


def kernel(sizes, clusters, cond_ref, label_ref, dens_ref, t_hbm, f_hbm, m_hbm, next_hbm, force_hbm,
           t_v, f_v, m_v, k_v, flux_v, hxs, hxr, hys, hyr, hzs, hzr, xm, ym, zm, xb, yb, zb, lab, cbuf,
           out_v, fout_v, in_sem, out_sem, hs_sem, hr_sem, *sems):
    nx, ny, nz = sizes
    me = {axis: lax.axis_index(axis) for axis in AXES}
    count = dict(zip(AXES, sizes))
    cz, cy, cx = 8, 16, 128
    lines = cz * cy

    def target(axes, index):
        ids = dict(me)
        for axis in reversed(axes):
            ids[axis] = lax.rem(index, count[axis])
            index = index // count[axis]
        return tuple(ids[axis] for axis in AXES)

    def place(axes):
        n, here = 1, 0
        for axis in axes:
            n, here = n * count[axis], here * count[axis] + me[axis]
        return n, here

    stages_c = [("gx", "gy")] if nx * ny <= 16 else [("gx",), ("gy",)]
    hxr[...] = jnp.zeros_like(hxr)
    hyr[...] = jnp.zeros_like(hyr)
    hzr[...] = jnp.zeros_like(hzr)
    barrier = pltpu.get_barrier_semaphore()
    greeted = 0
    plane = ("gx", "gy") if nx * ny <= 16 else None
    groups = [plane, ("gz",)] if plane else [("gx",), ("gy",), ("gz",)]
    for axes in groups:
        n, here = place(axes)
        for d in range(1, n):
            pl.semaphore_signal(barrier, inc=1, device_id=target(axes, lax.rem(here + d, n)),
                                device_id_type=MESH)
            greeted += 1
    ins = [pltpu.make_async_copy(s, d, in_sem.at[i])
           for i, (s, d) in enumerate(((m_hbm, m_v), (t_hbm, t_v), (f_hbm, f_v)))]
    for c in ins:
        c.start()

    finish = []

    class Gather:
        def __init__(self, buf, axes, ssem, rsem):
            self.buf, self.axes, self.ssem, self.rsem = buf, axes, ssem, rsem
            self.n, self.here = place(axes)

        def copy(self, d, slot):
            return pltpu.make_async_remote_copy(
                src_ref=self.buf.at[slot], dst_ref=self.buf.at[slot], send_sem=self.ssem.at[d - 1],
                recv_sem=self.rsem.at[slot], device_id=target(self.axes, lax.rem(self.here + d, self.n)),
                device_id_type=MESH)

        def start(self):
            for d in range(1, self.n):
                c = self.copy(d, self.here)
                c.start()
                finish.append(c)

        def wait(self):
            for d in range(1, self.n):
                self.copy(d, lax.rem(self.here + self.n - d, self.n)).wait_recv()

    gathers = []
    specs = [(xm, ("gx",)), (ym, ("gy",)), (zm, ("gz",)), (xb, ("gx",)), (yb, ("gy",)), (zb, ("gz",)),
             (lab, ("gz",))]
    for i, (buf, axes) in enumerate(specs):
        gathers.append(Gather(buf, axes, sems[2 * i], sems[2 * i + 1]))
    gxm, gym, gzm, gxb, gyb, gzb, glab = gathers

    rows8 = lax.broadcasted_iota(jnp.int32, (8, 128), 0)
    lanes8 = lax.broadcasted_iota(jnp.int32, (8, 128), 1)
    own_label = jnp.zeros((8, 128), jnp.float32)
    for t in range(8):
        own_label = jnp.where(rows8 == t, label_ref[0, t // 4, t % 4].astype(jnp.float32), own_label)
    lab[me["gz"]] = own_label

    ins[0].wait()
    material = m_v[...]
    k = jnp.zeros(material.shape, jnp.float32)
    for level in range(8):
        k = jnp.where(material == level, cond_ref[level], k)
    k_v[...] = k
    ins[1].wait()

    def yz(ref):
        return jnp.concatenate([ref[pl.ds(y, cz, stride=cy), :][None] for y in range(cy)], axis=0)

    k_yz, t_yz = yz(k_v), yz(t_v)
    k_x = k_yz.reshape(lines, cx).T
    t_x = t_yz.reshape(lines, cx).T
    k_zy, t_zy = k.reshape(cz, cy, cx), t_v[...].reshape(cz, cy, cx)
    for axis_k, axis_t, buf in ((k_x, t_x, hxs), (k_yz, t_yz, hys), (k_zy, t_zy, hzs)):
        n = axis_k.shape[0]
        for side, at in ((0, 0), (1, n - 1)):
            if axis_k.ndim == 2:
                buf[side, 0:1] = axis_k[at:at + 1]
                buf[side, 1:2] = axis_t[at:at + 1]
            else:
                buf[side, 0] = axis_k[at]
                buf[side, 1] = axis_t[at]

    pl.semaphore_wait(barrier, greeted)

    halos = []
    for i, (axis, sbuf, rbuf) in enumerate((("gx", hxs, hxr), ("gy", hys, hyr), ("gz", hzs, hzr))):
        n, here = count[axis], me[axis]
        for side in (0, 1):
            other = lax.rem(here + (1 if side else n - 1), n)
            c = pltpu.make_async_remote_copy(
                src_ref=sbuf.at[side], dst_ref=rbuf.at[1 - side], send_sem=hs_sem.at[2 * i + side],
                recv_sem=hr_sem.at[2 * i + 1 - side], device_id=target((axis,), other), device_id_type=MESH)
            r = pltpu.make_async_remote_copy(
                src_ref=sbuf.at[side], dst_ref=rbuf.at[side], send_sem=hs_sem.at[2 * i + side],
                recv_sem=hr_sem.at[2 * i + side], device_id=target((axis,), other), device_id_type=MESH)
            has = here < n - 1 if side else here > 0
            halos.append((has, c, r))
            pl.when(has)(c.start)
    glab.start()

    a_x = half_face(k_x, LATERAL_RATE)
    a_y = half_face(k_yz, LATERAL_RATE)
    a_z = half_face(k_zy, VERTICAL_RATE)

    def ends(first, last, kk, rate):
        n = first.shape[0]
        return (last[n - 1:] + 1.0 / (rate * kk[n - 1:]), first[:1] + 1.0 / (rate * kk[:1]), first[n - 1:])

    def put3(buf, here, parts):
        for i, part in enumerate(parts):
            if part.ndim == 2:
                buf[here, i:i + 1] = part
            else:
                buf[here, i] = part[0]

    def get(buf, i, j):
        return buf[i, j:j + 1] if len(buf.shape) == 3 else buf[i, j][None]

    stages_x, inv_x, first_x, last_x = factor(a_x)
    put3(xm, me["gx"], ends(first_x, last_x, k_x, LATERAL_RATE))
    gxm.start()

    def inner_flux(a, t):
        flow = 2.0 * a * (t - down(t, 1))
        return up(flow, 1) - flow

    ins[2].wait()
    flux_x = inner_flux(a_x, t_x)
    flux_y = inner_flux(a_y, t_yz) + 0.5 * yz(f_v)
    flux_z = inner_flux(a_z, t_zy)

    for has, c, r in halos:
        pl.when(has)(r.wait_recv)

    def halo_flux(k_own, t_own, k_far, t_far, rate):
        return 2.0 * rate * k_own * k_far / (k_own + k_far) * (t_far - t_own)

    def with_halo(flux, kk, tt, buf, rate):
        n = flux.shape[0]
        get_h = lambda side, j: buf[side, j:j + 1] if flux.ndim == 2 else buf[side, j][None]
        low = halo_flux(kk[:1], tt[:1], get_h(0, 0), get_h(0, 1), rate)
        high = halo_flux(kk[n - 1:], tt[n - 1:], get_h(1, 0), get_h(1, 1), rate)
        if flux.ndim == 2:
            rows = lax.broadcasted_iota(jnp.int32, flux.shape, 0)
            return flux + jnp.where(rows == 0, low, 0.0) + jnp.where(rows == n - 1, high, 0.0)
        return jnp.concatenate([flux[:1] + low, flux[1:n - 1], flux[n - 1:] + high], axis=0)

    flux_v[...] = with_halo(flux_z, k_zy, t_zy, hzr, VERTICAL_RATE).reshape(lines, cx)
    flux_y = with_halo(flux_y, k_yz, t_yz, hyr, LATERAL_RATE) + yz(flux_v)
    residual = with_halo(flux_x, k_x, t_x, hxr, LATERAL_RATE) + flux_y.reshape(lines, cx).T

    r_x = apply_stages(stages_x, inv_x, residual)
    put3(xb, me["gx"], (r_x[:1], r_x[cx - 1:]))
    gxb.start()

    stages_y, inv_y, first_y, last_y = factor(a_y)
    put3(ym, me["gy"], ends(first_y, last_y, k_yz, LATERAL_RATE))
    gym.start()
    gxm.wait()
    elim_x = chain_factor([tuple(get(xm, i, j) for j in range(3)) for i in range(nx)])
    gxb.wait()

    def join(buf, n, elim, r, first, last, here):
        qs = chain_flux(elim, [get(buf, i, 0) for i in range(n)], [get(buf, i, 1) for i in range(n)])
        if not qs:
            return r, qs
        return r + pick(qs, here - 1) * first - pick(qs, here) * last, qs

    step, _ = join(xb, nx, elim_x, r_x, first_x, last_x, me["gx"])
    r_y = apply_stages(stages_y, inv_y, step.T.reshape(cy, cz, cx))
    put3(yb, me["gy"], (r_y[:1], r_y[cy - 1:]))
    gyb.start()

    stages_z, inv_z, first_z, last_z = factor(a_z)
    put3(zm, me["gz"], ends(first_z, last_z, k_zy, VERTICAL_RATE))
    gzm.start()
    gym.wait()
    elim_y = chain_factor([tuple(get(ym, i, j) for j in range(3)) for i in range(ny)])
    gyb.wait()
    step, _ = join(yb, ny, elim_y, r_y, first_y, last_y, me["gy"])
    for y in range(cy):
        flux_v[pl.ds(y, cz, stride=cy), :] = step[y]
    rhs_z = flux_v[...].reshape(cz, cy, cx)
    r_z = apply_stages(stages_z, inv_z, rhs_z)
    put3(zb, me["gz"], (r_z[:1], r_z[cz - 1:], jnp.sum(t_zy + rhs_z, axis=0, keepdims=True)))
    gzb.start()

    gzm.wait()
    elim_z = chain_factor([tuple(get(zm, i, j) for j in range(3)) for i in range(nz)])
    glab.wait()
    width = cbuf.shape[-1] if len(cbuf.shape) == 3 else 128
    ids = lax.broadcasted_iota(jnp.int32, (8, width), 1).astype(jnp.float32)

    def onehot(labels):
        return jnp.concatenate([labels] * (width // 128), axis=1) == ids

    in_tile = lanes8 // TX == rows8 % 4
    gzb.wait()
    step, qs = join(zb, nz, elim_z, r_z, first_z, last_z, me["gz"])

    total = jnp.zeros((8, width), jnp.float32)
    for i in range(nz):
        cells = get(zb, i, 2)[0]
        if i > 0:
            cells = cells + qs[i - 1][0]
        if i < nz - 1:
            cells = cells - qs[i][0]
        upper = jnp.sum(cells[:TY], axis=0, keepdims=True)
        lower = jnp.sum(cells[TY:], axis=0, keepdims=True)
        tiles = jnp.where(in_tile, jnp.where(rows8 < 4, upper, lower), 0.0)
        sums = jnp.sum(tiles, axis=1, keepdims=True)
        total = total + jnp.where(onehot(lab[i]), sums, 0.0)
    total = jnp.sum(total, axis=0, keepdims=True)
    base = 0
    for j, axes in enumerate(stages_c):
        n, here = place(axes)
        part = Gather(cbuf.at[pl.ds(base, n)], axes, sems[14 + 2 * j], sems[15 + 2 * j])
        cbuf[base + here, 0:1] = total
        part.start()
        if j == 0:
            out_v[...] = (t_zy + step).reshape(lines, cx)
            out0 = pltpu.make_async_copy(out_v, next_hbm, out_sem.at[0])
            out0.start()
        part.wait()
        total = cbuf[base, 0:1]
        for i in range(1, n):
            total = total + cbuf[base + i, 0:1]
        base += n

    mean = total / (4 * cz * TY * TX)
    leak = dens_ref[...] * jnp.exp(LEAK_SLOPE * mean[:, :clusters])
    power = jnp.sum(jnp.where(onehot(own_label)[:, :clusters], leak, 0.0), axis=1, keepdims=True)
    spread = jnp.where(in_tile, power, 0.0)
    upper = jnp.sum(spread[:4], axis=0, keepdims=True)
    lower = jnp.sum(spread[4:], axis=0, keepdims=True)
    rows16 = lax.broadcasted_iota(jnp.int32, (cy, cx), 0)
    layer = jnp.where(rows16 < TY, upper, lower)
    fout_v[...] = (f_v[...].reshape(cz, cy, cx) + layer[None]).reshape(lines, cx)
    out1 = pltpu.make_async_copy(fout_v, force_hbm, out_sem.at[1])
    out1.start()

    for has, c, r in halos:
        pl.when(has)(c.wait_send)
    for c in finish:
        c.wait_send()
    out0.wait()
    out1.wait()


def per_device(sizes, thermal_field, forcing_per_step, substance_label, thermal_conductivities,
               patch_group_label, drain_power_density):
    nx, ny, nz = sizes
    shape = thermal_field.shape
    cz, cy, cx = shape
    lines = cz * cy
    clusters = drain_power_density.shape[0]
    width = -(-clusters // 128) * 128
    f32 = jnp.float32
    flat = lambda v: v.reshape(lines, cx)
    vm = lambda *s: pltpu.VMEM(s, f32)
    dma = pltpu.SemaphoreType.DMA
    small = nx * ny <= 16
    csizes = [nx * ny] if small else [nx, ny]
    sems = []
    for n in [nx, ny, nz, nx, ny, nz, nz] + csizes:
        sems += [dma((max(n - 1, 1),)), dma((n,))]
    any_spec = pl.BlockSpec(memory_space=pl.ANY)
    smem = pl.BlockSpec(memory_space=pltpu.SMEM)
    new, force = pl.pallas_call(
        functools.partial(kernel, sizes, clusters),
        out_shape=[jax.ShapeDtypeStruct((lines, cx), f32)] * 2,
        in_specs=[smem, smem, pl.BlockSpec(memory_space=pltpu.VMEM), any_spec, any_spec, any_spec],
        out_specs=[any_spec, any_spec],
        scratch_shapes=[
            vm(lines, cx), vm(lines, cx), pltpu.VMEM((lines, cx), jnp.int32), vm(lines, cx), vm(lines, cx),
            vm(2, 2, lines), vm(2, 2, lines), vm(2, 2, cz, cx), vm(2, 2, cz, cx), vm(2, 2, cy, cx), vm(2, 2, cy, cx),
            vm(nx, 8, lines), vm(ny, 3, cz, cx), vm(nz, 3, cy, cx),
            vm(nx, 8, lines), vm(ny, 2, cz, cx), vm(nz, 3, cy, cx),
            vm(nz, 8, 128), vm(sum(csizes), 8, width),
            vm(lines, cx), vm(lines, cx),
            dma((3,)), dma((2,)), dma((6,)), dma((6,)),
        ] + sems,
        compiler_params=pltpu.CompilerParams(collective_id=0, has_side_effects=True),
    )(thermal_conductivities, patch_group_label, drain_power_density.reshape(1, clusters),
      flat(thermal_field), flat(forcing_per_step), flat(substance_label))
    return new.reshape(shape), force.reshape(shape)


def solution(mesh):
    block = P("gz", "gy", "gx")
    return jax.shard_map(
        functools.partial(per_device, tuple(mesh.shape[axis] for axis in AXES)),
        mesh=mesh, in_specs=(block, block, block, P(), block, P()), out_specs=(block, block), check_vma=False,
    )
```

time: 111 us -> 26 us (0.23)
  blocking collectives: 61.8 us -> 0 us
  Pallas kernels: 0 us -> 23 us
  starting transfers between devices: 13.5 us -> 0 us
  other arithmetic: 12.2 us -> 0 us
  waiting for transfers between devices: 11.7 us -> 0 us
  local copies, waits for them, and re-layouts: 8.1 us -> 2.14 us
  between operations: 1.81 us -> 0.65 us
    psum x1 -> x0, blocking collectives: 37.5 us -> none  [per_device(): cluster_total = lax.psum(partial_value, ('gx', 'gy', 'gz'))]
    all_gather x3 -> x0, blocking collectives: 24.3 us -> none  [the longest x1 13.8 us: interface_z(): gathered = lax.all_gather(coeffs[None], 'gz', axis=0, tiled=True)]
    pallas_call x0 -> x1, Pallas kernels: none -> 23 us  [per_device(): pl.pallas_call(functools.partial(kernel, sizes, clusters), out_shape=[jax...]
    ppermute x6 -> x0, starting transfers between devices: 13.5 us -> none  [the longest x3 9.62 us: padded(): before = lax.ppermute(last, axis, up)]
    ppermute x6 -> x0, waiting for transfers between devices: 11.7 us -> none  [the longest x3 10.3 us: padded(): after = lax.ppermute(first, axis, down)]
    another operation x2 -> x0, other arithmetic: 6.03 us -> none  [per_device(): joined_outputs = jnp.stack([thermal_field, voxel_thermal_link])]
    slice x87 -> x0, local copies, waits for them, and re-layouts: 5.86 us -> none  [the longest x50 2.41 us: shifted(): lax.slice_in_dim(values, 0, length - offset, axis=axis)]
    add x36 -> x0, other arithmetic: 3.58 us -> none  [the longest x14 1.78 us: reduce_lines(): source + factor_down * shifted(source, stride, axis, 0.0)]
  transfers between devices with their start and end apart: 6 -> 0, of which waited for: 4 -> 0; matrix products, arithmetic and copies ran while one was open for 0% -> 0% of each run, Pallas kernels for 0% -> 0%
where the time goes in v1:
time: 26 us; the launch traced here: 25.7 us
  Pallas kernels  23 us (88%)
  local copies, waits for them, and re-layouts  2.14 us (8%)
  between operations  0.65 us (2%)
    pallas_call x1, Pallas kernels, per_device(): pl.pallas_call(functools.partial(kernel, sizes, clusters), out_shape=[jax...  23 us
    unnamed x4, local copies, waits for them, and re-layouts  2.14 us

profile of v1, /device:TPU:0, one launch (start us, length us, event | category | flops | bytes accessed | tf_op | source)
XLA Modules:
  0.0 25.7 jit_solution(8064209448914078470)
XLA Ops:
  0.6 23.0 %shard_map.77 = (f32[128,128]{1,0:T(8,128)}, f32[128,128]{1,0:T(8,128)}) custom-call(f32[8]{0:T(128)} %cond_ref.1, s32[1,2,4]{2,1,0:T(2,128)} %label_ref.1, f32[1,64]{1,0:T(1,128)} %bitcast.11, f32[128,128]{1,0:T(8,128)} %bitcast.6, f32[128,128]{1,0:T(8,128)} %bitcast.7, s32[128,128]{1,0:T(8,128)} %bitcast.8), custom_call_target="tpu_custom_call" | custom-call | tf_op jit(solution)/shard_map/pallas_call | solution.py:391
  23.6 0.0 copy-start
  23.6 1.5 %copy.10 = f32[8,16,128]{2,1,0:T(8,128)} copy(f32[8,16,128]{2,1,0:T(8,128)} %bitcast.10) | data formatting | bytes 131072
  25.1 0.0 copy-done
  25.1 0.6 %copy.11 = f32[8,16,128]{2,1,0:T(8,128)} copy(f32[8,16,128]{2,1,0:T(8,128)S(1)} %bitcast.9) | data formatting | bytes 131072
Async XLA Ops:
  23.6 1.5 %copy-start = (f32[128,128]{1,0:T(8,128)S(1)}, f32[128,128]{1,0:T(8,128)}, u32[]{:S(2)}) copy-start(f32[128,128]{1,0:T(8,128)} %get-tuple-element.5) | copy-start | bytes 196612

commit v2 on v1

--- a/solution.py
+++ b/solution.py
@@ -74,7 +74,7 @@
         if slope is not None:
             den = den - mats[i][2] * slope
         inv = 1.0 / den
-        slope = mats[i + 1][2] * inv
+        slope = mats[i + 1][2] * inv if i < len(mats) - 2 else None
         out.append((inv, slope, mats[i][2]))
     return out
 
@@ -99,9 +99,9 @@
     return out
 
 
-def kernel(sizes, clusters, cond_ref, label_ref, dens_ref, t_hbm, f_hbm, m_hbm, next_hbm, force_hbm,
-           t_v, f_v, m_v, k_v, flux_v, hxs, hxr, hys, hyr, hzs, hzr, xm, ym, zm, xb, yb, zb, lab, cbuf,
-           out_v, fout_v, in_sem, out_sem, hs_sem, hr_sem, *sems):
+def kernel(sizes, clusters, cond_ref, label_ref, dens_ref, t_hbm, f_hbm, m_hbm, next_ref, force_ref,
+           t_v, f_v, m_v, k_v, flux_v, hys, hyr, hzs, hzr, xm, ym, zm, xb, yb, zb, lab, cbuf,
+           in_sem, hs_sem, hr_sem, relay_x, relay_z, *sems):
     nx, ny, nz = sizes
     me = {axis: lax.axis_index(axis) for axis in AXES}
     count = dict(zip(AXES, sizes))
@@ -122,19 +122,34 @@
         return n, here
 
     stages_c = [("gx", "gy")] if nx * ny <= 16 else [("gx",), ("gy",)]
-    hxr[...] = jnp.zeros_like(hxr)
     hyr[...] = jnp.zeros_like(hyr)
     hzr[...] = jnp.zeros_like(hzr)
     barrier = pltpu.get_barrier_semaphore()
     greeted = 0
-    plane = ("gx", "gy") if nx * ny <= 16 else None
-    groups = [plane, ("gz",)] if plane else [("gx",), ("gy",), ("gz",)]
-    for axes in groups:
-        n, here = place(axes)
-        for d in range(1, n):
-            pl.semaphore_signal(barrier, inc=1, device_id=target(axes, lax.rem(here + d, n)),
-                                device_id_type=MESH)
-            greeted += 1
+
+    def greet(axes, index):
+        pl.semaphore_signal(barrier, inc=1, device_id=target(axes, index), device_id_type=MESH)
+
+    square = nx == 4
+    partners_x = [me["gx"] + 1 - 2 * lax.rem(me["gx"], 2), lax.rem(me["gx"] + 2, nx)] if square else [
+        lax.rem(me["gx"] + d, nx) for d in range(1, nx)]
+    for index in partners_x:
+        greet(("gx",), index)
+    for d in range(1, ny):
+        greet(("gy",), lax.rem(me["gy"] + d, ny))
+    greeted = len(partners_x) + ny - 1
+    below_z, above_z = me["gz"] > 0, me["gz"] < nz - 1
+    near_z = ((below_z, lax.rem(me["gz"] + nz - 1, nz)), (above_z, lax.rem(me["gz"] + 1, nz)))
+    line_z = nz <= 4
+    if line_z:
+        for has, index in near_z:
+            pl.when(has)(functools.partial(greet, ("gz",), index))
+        count_z = jnp.where(below_z, 1, 0) + jnp.where(above_z, 1, 0)
+        greeted = greeted + count_z
+    else:
+        for d in range(1, nz):
+            greet(("gz",), lax.rem(me["gz"] + d, nz))
+        greeted += nz - 1
     ins = [pltpu.make_async_copy(s, d, in_sem.at[i])
            for i, (s, d) in enumerate(((m_hbm, m_v), (t_hbm, t_v), (f_hbm, f_v)))]
     for c in ins:
@@ -143,31 +158,47 @@
     finish = []
 
     class Gather:
-        def __init__(self, buf, axes, ssem, rsem):
-            self.buf, self.axes, self.ssem, self.rsem = buf, axes, ssem, rsem
+        def __init__(self, buf, axes, ssem, rsem, edge=None):
+            self.buf, self.axes, self.ssem, self.rsem, self.edge = buf, axes, ssem, rsem, edge
             self.n, self.here = place(axes)
 
-        def copy(self, d, slot):
-            return pltpu.make_async_remote_copy(
-                src_ref=self.buf.at[slot], dst_ref=self.buf.at[slot], send_sem=self.ssem.at[d - 1],
-                recv_sem=self.rsem.at[slot], device_id=target(self.axes, lax.rem(self.here + d, self.n)),
-                device_id_type=MESH)
+        def copies(self, d, slot):
+            def make(ref):
+                return pltpu.make_async_remote_copy(
+                    src_ref=ref, dst_ref=ref, send_sem=self.ssem.at[d - 1], recv_sem=self.rsem.at[slot],
+                    device_id=target(self.axes, lax.rem(self.here + d, self.n)), device_id_type=MESH)
+            if self.edge is None:
+                return [(None, make(self.buf.at[slot]))]
+            rows, offset = self.edge
+            first, last = slot == 0, slot == self.n - 1
+            return [(first, make(self.buf.at[slot, pl.ds(offset, rows)])),
+                    (last, make(self.buf.at[slot, pl.ds(0, rows)])),
+                    (jnp.logical_not(first | last), make(self.buf.at[slot]))]
+
+        @staticmethod
+        def do(has, action):
+            if has is None:
+                action()
+            else:
+                pl.when(has)(action)
 
         def start(self):
             for d in range(1, self.n):
-                c = self.copy(d, self.here)
-                c.start()
-                finish.append(c)
+                for has, c in self.copies(d, self.here):
+                    self.do(has, c.start)
+                    finish.append((has, c))
 
         def wait(self):
             for d in range(1, self.n):
-                self.copy(d, lax.rem(self.here + self.n - d, self.n)).wait_recv()
+                for has, c in self.copies(d, lax.rem(self.here + self.n - d, self.n)):
+                    self.do(has, c.wait_recv)
 
     gathers = []
     specs = [(xm, ("gx",)), (ym, ("gy",)), (zm, ("gz",)), (xb, ("gx",)), (yb, ("gy",)), (zb, ("gz",)),
              (lab, ("gz",))]
     for i, (buf, axes) in enumerate(specs):
-        gathers.append(Gather(buf, axes, sems[2 * i], sems[2 * i + 1]))
+        edge = {2: (16, 32), 5: (24, 16)}.get(i)
+        gathers.append(Gather(buf, axes, sems[2 * i], sems[2 * i + 1], edge))
     gxm, gym, gzm, gxb, gyb, gzb, glab = gathers
 
     rows8 = lax.broadcasted_iota(jnp.int32, (8, 128), 0)
@@ -189,23 +220,19 @@
         return jnp.concatenate([ref[pl.ds(y, cz, stride=cy), :][None] for y in range(cy)], axis=0)
 
     k_yz, t_yz = yz(k_v), yz(t_v)
-    k_x = k_yz.reshape(lines, cx).T
-    t_x = t_yz.reshape(lines, cx).T
     k_zy, t_zy = k.reshape(cz, cy, cx), t_v[...].reshape(cz, cy, cx)
-    for axis_k, axis_t, buf in ((k_x, t_x, hxs), (k_yz, t_yz, hys), (k_zy, t_zy, hzs)):
+    for axis_k, axis_t, buf in ((k_yz, t_yz, hys), (k_zy, t_zy, hzs)):
         n = axis_k.shape[0]
         for side, at in ((0, 0), (1, n - 1)):
-            if axis_k.ndim == 2:
-                buf[side, 0:1] = axis_k[at:at + 1]
-                buf[side, 1:2] = axis_t[at:at + 1]
-            else:
-                buf[side, 0] = axis_k[at]
-                buf[side, 1] = axis_t[at]
+            buf[side, 0] = axis_k[at]
+            buf[side, 1] = axis_t[at]
 
     pl.semaphore_wait(barrier, greeted)
+    if square:
+        pl.semaphore_signal(relay_x, inc=1, device_id=target(("gx",), partners_x[0]), device_id_type=MESH)
 
     halos = []
-    for i, (axis, sbuf, rbuf) in enumerate((("gx", hxs, hxr), ("gy", hys, hyr), ("gz", hzs, hzr))):
+    for i, (axis, sbuf, rbuf) in enumerate((("gz", hzs, hzr), ("gy", hys, hyr))):
         n, here = count[axis], me[axis]
         for side in (0, 1):
             other = lax.rem(here + (1 if side else n - 1), n)
@@ -218,7 +245,8 @@
             has = here < n - 1 if side else here > 0
             halos.append((has, c, r))
             pl.when(has)(c.start)
-    glab.start()
+    k_x = k_yz.reshape(lines, cx).T
+    t_x = t_yz.reshape(lines, cx).T
 
     a_x = half_face(k_x, LATERAL_RATE)
     a_y = half_face(k_yz, LATERAL_RATE)
@@ -240,6 +268,8 @@
 
     stages_x, inv_x, first_x, last_x = factor(a_x)
     put3(xm, me["gx"], ends(first_x, last_x, k_x, LATERAL_RATE))
+    if square:
+        pl.semaphore_wait(relay_x, 1)
     gxm.start()
 
     def inner_flux(a, t):
@@ -253,39 +283,49 @@
 
     for has, c, r in halos:
         pl.when(has)(r.wait_recv)
+    if line_z:
+        for has, index in near_z:
+            pl.when(has)(functools.partial(pl.semaphore_signal, relay_z, inc=1, device_id=target(("gz",), index),
+                                           device_id_type=MESH))
 
     def halo_flux(k_own, t_own, k_far, t_far, rate):
         return 2.0 * rate * k_own * k_far / (k_own + k_far) * (t_far - t_own)
 
     def with_halo(flux, kk, tt, buf, rate):
         n = flux.shape[0]
-        get_h = lambda side, j: buf[side, j:j + 1] if flux.ndim == 2 else buf[side, j][None]
-        low = halo_flux(kk[:1], tt[:1], get_h(0, 0), get_h(0, 1), rate)
-        high = halo_flux(kk[n - 1:], tt[n - 1:], get_h(1, 0), get_h(1, 1), rate)
-        if flux.ndim == 2:
-            rows = lax.broadcasted_iota(jnp.int32, flux.shape, 0)
-            return flux + jnp.where(rows == 0, low, 0.0) + jnp.where(rows == n - 1, high, 0.0)
+        low = halo_flux(kk[:1], tt[:1], buf[0, 0][None], buf[0, 1][None], rate)
+        high = halo_flux(kk[n - 1:], tt[n - 1:], buf[1, 0][None], buf[1, 1][None], rate)
         return jnp.concatenate([flux[:1] + low, flux[1:n - 1], flux[n - 1:] + high], axis=0)
 
     flux_v[...] = with_halo(flux_z, k_zy, t_zy, hzr, VERTICAL_RATE).reshape(lines, cx)
     flux_y = with_halo(flux_y, k_yz, t_yz, hyr, LATERAL_RATE) + yz(flux_v)
-    residual = with_halo(flux_x, k_x, t_x, hxr, LATERAL_RATE) + flux_y.reshape(lines, cx).T
+    residual = flux_x + flux_y.reshape(lines, cx).T
 
     r_x = apply_stages(stages_x, inv_x, residual)
-    put3(xb, me["gx"], (r_x[:1], r_x[cx - 1:]))
+    put3(xb, me["gx"], (r_x[:1] + 2.0 * t_x[:1], r_x[cx - 1:] + 2.0 * t_x[cx - 1:]))
     gxb.start()
 
     stages_y, inv_y, first_y, last_y = factor(a_y)
     put3(ym, me["gy"], ends(first_y, last_y, k_yz, LATERAL_RATE))
     gym.start()
+    stages_z, inv_z, first_z, last_z = factor(a_z)
+    high_z, low_z, cross_z = ends(first_z, last_z, k_zy, VERTICAL_RATE)
+    for i, part in enumerate((low_z, cross_z, high_z)):
+        zm[me["gz"], i * cy:(i + 1) * cy] = part[0]
+    if line_z:
+        pl.semaphore_wait(relay_z, count_z)
+    gzm.start()
+    glab.start()
     gxm.wait()
     elim_x = chain_factor([tuple(get(xm, i, j) for j in range(3)) for i in range(nx)])
     gxb.wait()
 
     def join(buf, n, elim, r, first, last, here):
-        qs = chain_flux(elim, [get(buf, i, 0) for i in range(n)], [get(buf, i, 1) for i in range(n)])
-        if not qs:
-            return r, qs
+        if buf is zb:
+            firsts, lasts = [zb[i, :cy][None] for i in range(n)], [zb[i, 24:40][None] for i in range(n)]
+        else:
+            firsts, lasts = [get(buf, i, 0) for i in range(n)], [get(buf, i, 1) for i in range(n)]
+        qs = chain_flux(elim, firsts, lasts)
         return r + pick(qs, here - 1) * first - pick(qs, here) * last, qs
 
     step, _ = join(xb, nx, elim_x, r_x, first_x, last_x, me["gx"])
@@ -293,9 +333,6 @@
     put3(yb, me["gy"], (r_y[:1], r_y[cy - 1:]))
     gyb.start()
 
-    stages_z, inv_z, first_z, last_z = factor(a_z)
-    put3(zm, me["gz"], ends(first_z, last_z, k_zy, VERTICAL_RATE))
-    gzm.start()
     gym.wait()
     elim_y = chain_factor([tuple(get(ym, i, j) for j in range(3)) for i in range(ny)])
     gyb.wait()
@@ -304,11 +341,15 @@
         flux_v[pl.ds(y, cz, stride=cy), :] = step[y]
     rhs_z = flux_v[...].reshape(cz, cy, cx)
     r_z = apply_stages(stages_z, inv_z, rhs_z)
-    put3(zb, me["gz"], (r_z[:1], r_z[cz - 1:], jnp.sum(t_zy + rhs_z, axis=0, keepdims=True)))
+    zb[me["gz"], 0:cy] = r_z[0]
+    zb[me["gz"], 24:40] = r_z[cz - 1]
+    columns = jnp.sum(t_zy + rhs_z, axis=0)
+    for i in range(cy // TY):
+        zb[me["gz"], 16 + i:17 + i] = jnp.sum(columns[i * TY:(i + 1) * TY], axis=0, keepdims=True)
     gzb.start()
 
     gzm.wait()
-    elim_z = chain_factor([tuple(get(zm, i, j) for j in range(3)) for i in range(nz)])
+    elim_z = chain_factor([tuple(zm[i, j * cy:(j + 1) * cy][None] for j in (2, 0, 1)) for i in range(nz)])
     glab.wait()
     width = cbuf.shape[-1] if len(cbuf.shape) == 3 else 128
     ids = lax.broadcasted_iota(jnp.int32, (8, width), 1).astype(jnp.float32)
@@ -322,13 +363,13 @@
 
     total = jnp.zeros((8, width), jnp.float32)
     for i in range(nz):
-        cells = get(zb, i, 2)[0]
+        cells = jnp.zeros((cy, cx), jnp.float32)
         if i > 0:
             cells = cells + qs[i - 1][0]
         if i < nz - 1:
             cells = cells - qs[i][0]
-        upper = jnp.sum(cells[:TY], axis=0, keepdims=True)
-        lower = jnp.sum(cells[TY:], axis=0, keepdims=True)
+        upper = zb[i, 16:17] + jnp.sum(cells[:TY], axis=0, keepdims=True)
+        lower = zb[i, 17:18] + jnp.sum(cells[TY:], axis=0, keepdims=True)
         tiles = jnp.where(in_tile, jnp.where(rows8 < 4, upper, lower), 0.0)
         sums = jnp.sum(tiles, axis=1, keepdims=True)
         total = total + jnp.where(onehot(lab[i]), sums, 0.0)
@@ -340,9 +381,7 @@
         cbuf[base + here, 0:1] = total
         part.start()
         if j == 0:
-            out_v[...] = (t_zy + step).reshape(lines, cx)
-            out0 = pltpu.make_async_copy(out_v, next_hbm, out_sem.at[0])
-            out0.start()
+            next_ref[...] = (t_zy + step).reshape(lines, cx)
         part.wait()
         total = cbuf[base, 0:1]
         for i in range(1, n):
@@ -357,16 +396,12 @@
     lower = jnp.sum(spread[4:], axis=0, keepdims=True)
     rows16 = lax.broadcasted_iota(jnp.int32, (cy, cx), 0)
     layer = jnp.where(rows16 < TY, upper, lower)
-    fout_v[...] = (f_v[...].reshape(cz, cy, cx) + layer[None]).reshape(lines, cx)
-    out1 = pltpu.make_async_copy(fout_v, force_hbm, out_sem.at[1])
-    out1.start()
+    force_ref[...] = (f_v[...].reshape(cz, cy, cx) + layer[None]).reshape(lines, cx)
 
     for has, c, r in halos:
         pl.when(has)(c.wait_send)
-    for c in finish:
-        c.wait_send()
-    out0.wait()
-    out1.wait()
+    for has, c in finish:
+        Gather.do(has, c.wait_send)
 
 
 def per_device(sizes, thermal_field, forcing_per_step, substance_label, thermal_conductivities,
@@ -390,17 +425,16 @@
     smem = pl.BlockSpec(memory_space=pltpu.SMEM)
     new, force = pl.pallas_call(
         functools.partial(kernel, sizes, clusters),
-        out_shape=[jax.ShapeDtypeStruct((lines, cx), f32)] * 2,
+        out_shape=[pltpu.VMEM((lines, cx), f32)] * 2,
         in_specs=[smem, smem, pl.BlockSpec(memory_space=pltpu.VMEM), any_spec, any_spec, any_spec],
-        out_specs=[any_spec, any_spec],
+        out_specs=[pl.BlockSpec(memory_space=pltpu.VMEM)] * 2,
         scratch_shapes=[
             vm(lines, cx), vm(lines, cx), pltpu.VMEM((lines, cx), jnp.int32), vm(lines, cx), vm(lines, cx),
-            vm(2, 2, lines), vm(2, 2, lines), vm(2, 2, cz, cx), vm(2, 2, cz, cx), vm(2, 2, cy, cx), vm(2, 2, cy, cx),
-            vm(nx, 8, lines), vm(ny, 3, cz, cx), vm(nz, 3, cy, cx),
-            vm(nx, 8, lines), vm(ny, 2, cz, cx), vm(nz, 3, cy, cx),
-            vm(nz, 8, 128), vm(sum(csizes), 8, width),
-            vm(lines, cx), vm(lines, cx),
-            dma((3,)), dma((2,)), dma((6,)), dma((6,)),
+            vm(2, 2, cz, cx), vm(2, 2, cz, cx), vm(2, 2, cy, cx), vm(2, 2, cy, cx),
+            vm(nx, 8, lines), vm(ny, 3, cz, cx), vm(nz, 48, cx),
+            vm(nx, 8, lines), vm(ny, 2, cz, cx), vm(nz, 40, cx),
+            vm(nz, 8, 128), vm(sum(csizes), 1, width),
+            dma((3,)), dma((4,)), dma((4,)), pltpu.SemaphoreType.REGULAR, pltpu.SemaphoreType.REGULAR,
         ] + sems,
         compiler_params=pltpu.CompilerParams(collective_id=0, has_side_effects=True),
     )(thermal_conductivities, patch_group_label, drain_power_density.reshape(1, clusters),

time: 26 us -> 21.5 us (0.83)
  Pallas kernels: 23 us -> 19.4 us
  local copies, waits for them, and re-layouts: 2.14 us -> 1.26 us
    pallas_call x1, Pallas kernels: 23 us -> 19.4 us  [per_device(): pl.pallas_call(functools.partial(kernel, sizes, clusters), out_shape=[plt...]
    unnamed x4 -> x2, local copies, waits for them, and re-layouts: 2.14 us -> 1.26 us
where the time goes in v2:
time: 21.5 us; the launch traced here: 21.3 us
  Pallas kernels  19.4 us (90%)
  local copies, waits for them, and re-layouts  1.26 us (6%)
  between operations  0.64 us (3%)
    pallas_call x1, Pallas kernels, per_device(): pl.pallas_call(functools.partial(kernel, sizes, clusters), out_shape=[plt...  19.4 us
    unnamed x2, local copies, waits for them, and re-layouts  1.26 us

profile of v2, /device:TPU:0, one launch (start us, length us, event | category | flops | bytes accessed | tf_op | source)
XLA Modules:
  0.0 21.3 jit_solution(9741962600798624502)
XLA Ops:
  0.6 19.4 %shard_map.77 = (f32[128,128]{1,0:T(8,128)S(1)}, f32[128,128]{1,0:T(8,128)S(1)}) custom-call(f32[8]{0:T(128)} %cond_ref.1, s32[1,2,4]{2,1,0:T(2,128)} %label_ref.1, f32[1,64]{1,0:T(1,128)} %bitcast.11, f32[128,128]{1,0:T(8,128)} %bitcast.8, f32[128,128]{1,0:T(8,128)} %bitcast.9, s32[128,128]{1,0:T(8,128)} %bitcast.10), custom_call_target="tpu_custom_call" | custom-call | tf_op jit(solution)/shard_map/pallas_call | solution.py:426
  20.1 0.6 %copy.10 = f32[8,16,128]{2,1,0:T(8,128)} copy(f32[8,16,128]{2,1,0:T(8,128)S(1)} %bitcast.7) | data formatting | bytes 131072
  20.7 0.6 %copy.11 = f32[8,16,128]{2,1,0:T(8,128)} copy(f32[8,16,128]{2,1,0:T(8,128)S(1)} %bitcast.6) | data formatting | bytes 131072

commit v3 on v2

--- a/solution.py
+++ b/solution.py
@@ -99,8 +99,8 @@
     return out
 
 
-def kernel(sizes, clusters, cond_ref, label_ref, dens_ref, t_hbm, f_hbm, m_hbm, next_ref, force_ref,
-           t_v, f_v, m_v, k_v, flux_v, hys, hyr, hzs, hzr, xm, ym, zm, xb, yb, zb, lab, cbuf,
+def kernel(sizes, clusters, cond_hbm, label_hbm, dens_hbm, t_hbm, f_hbm, m_hbm, next_ref, force_ref,
+           cond_ref, label_ref, dens_ref, t_v, f_v, m_v, k_v, flux_v, hys, hyr, hzs, hzr, xm, ym, zm, xb, yb, zb, lab, cbuf,
            in_sem, hs_sem, hr_sem, relay_x, relay_z, *sems):
     nx, ny, nz = sizes
     me = {axis: lax.axis_index(axis) for axis in AXES}
@@ -151,9 +151,10 @@
             greet(("gz",), lax.rem(me["gz"] + d, nz))
         greeted += nz - 1
     ins = [pltpu.make_async_copy(s, d, in_sem.at[i])
-           for i, (s, d) in enumerate(((m_hbm, m_v), (t_hbm, t_v), (f_hbm, f_v)))]
-    for c in ins:
-        c.start()
+           for i, (s, d) in enumerate((
+               (m_hbm, m_v), (t_hbm, t_v), (f_hbm, f_v), (cond_hbm, cond_ref), (label_hbm, label_ref), (dens_hbm, dens_ref)))]
+    for i in (3, 0, 1, 4, 2, 5):
+        ins[i].start()
 
     finish = []
 
@@ -201,13 +202,7 @@
         gathers.append(Gather(buf, axes, sems[2 * i], sems[2 * i + 1], edge))
     gxm, gym, gzm, gxb, gyb, gzb, glab = gathers
 
-    rows8 = lax.broadcasted_iota(jnp.int32, (8, 128), 0)
-    lanes8 = lax.broadcasted_iota(jnp.int32, (8, 128), 1)
-    own_label = jnp.zeros((8, 128), jnp.float32)
-    for t in range(8):
-        own_label = jnp.where(rows8 == t, label_ref[0, t // 4, t % 4].astype(jnp.float32), own_label)
-    lab[me["gz"]] = own_label
-
+    ins[3].wait()
     ins[0].wait()
     material = m_v[...]
     k = jnp.zeros(material.shape, jnp.float32)
@@ -245,6 +240,14 @@
             has = here < n - 1 if side else here > 0
             halos.append((has, c, r))
             pl.when(has)(c.start)
+    ins[4].wait()
+    rows8 = lax.broadcasted_iota(jnp.int32, (8, 128), 0)
+    lanes8 = lax.broadcasted_iota(jnp.int32, (8, 128), 1)
+    own_label = jnp.zeros((8, 128), jnp.float32)
+    for t in range(8):
+        own_label = jnp.where(rows8 == t, label_ref[0, t // 4, t % 4].astype(jnp.float32), own_label)
+    lab[me["gz"]] = own_label
+
     k_x = k_yz.reshape(lines, cx).T
     t_x = t_yz.reshape(lines, cx).T
 
@@ -277,10 +280,18 @@
         return up(flow, 1) - flow
 
     ins[2].wait()
+    ins[5].wait()
     flux_x = inner_flux(a_x, t_x)
     flux_y = inner_flux(a_y, t_yz) + 0.5 * yz(f_v)
     flux_z = inner_flux(a_z, t_zy)
 
+    stages_z, inv_z, first_z, last_z = factor(a_z)
+    high_z, low_z, cross_z = ends(first_z, last_z, k_zy, VERTICAL_RATE)
+    for i, part in enumerate((low_z, cross_z, high_z)):
+        zm[me["gz"], i * cy:(i + 1) * cy] = part[0]
+    stages_y, inv_y, first_y, last_y = factor(a_y)
+    put3(ym, me["gy"], ends(first_y, last_y, k_yz, LATERAL_RATE))
+    gym.start()
     for has, c, r in halos:
         pl.when(has)(r.wait_recv)
     if line_z:
@@ -305,13 +316,6 @@
     put3(xb, me["gx"], (r_x[:1] + 2.0 * t_x[:1], r_x[cx - 1:] + 2.0 * t_x[cx - 1:]))
     gxb.start()
 
-    stages_y, inv_y, first_y, last_y = factor(a_y)
-    put3(ym, me["gy"], ends(first_y, last_y, k_yz, LATERAL_RATE))
-    gym.start()
-    stages_z, inv_z, first_z, last_z = factor(a_z)
-    high_z, low_z, cross_z = ends(first_z, last_z, k_zy, VERTICAL_RATE)
-    for i, part in enumerate((low_z, cross_z, high_z)):
-        zm[me["gz"], i * cy:(i + 1) * cy] = part[0]
     if line_z:
         pl.semaphore_wait(relay_z, count_z)
     gzm.start()
@@ -422,19 +426,20 @@
     for n in [nx, ny, nz, nx, ny, nz, nz] + csizes:
         sems += [dma((max(n - 1, 1),)), dma((n,))]
     any_spec = pl.BlockSpec(memory_space=pl.ANY)
-    smem = pl.BlockSpec(memory_space=pltpu.SMEM)
     new, force = pl.pallas_call(
         functools.partial(kernel, sizes, clusters),
         out_shape=[pltpu.VMEM((lines, cx), f32)] * 2,
-        in_specs=[smem, smem, pl.BlockSpec(memory_space=pltpu.VMEM), any_spec, any_spec, any_spec],
+        in_specs=[any_spec] * 6,
         out_specs=[pl.BlockSpec(memory_space=pltpu.VMEM)] * 2,
         scratch_shapes=[
+            pltpu.SMEM(thermal_conductivities.shape, f32), pltpu.SMEM(patch_group_label.shape, jnp.int32),
+            vm(1, clusters),
             vm(lines, cx), vm(lines, cx), pltpu.VMEM((lines, cx), jnp.int32), vm(lines, cx), vm(lines, cx),
             vm(2, 2, cz, cx), vm(2, 2, cz, cx), vm(2, 2, cy, cx), vm(2, 2, cy, cx),
             vm(nx, 8, lines), vm(ny, 3, cz, cx), vm(nz, 48, cx),
             vm(nx, 8, lines), vm(ny, 2, cz, cx), vm(nz, 40, cx),
             vm(nz, 8, 128), vm(sum(csizes), 1, width),
-            dma((3,)), dma((4,)), dma((4,)), pltpu.SemaphoreType.REGULAR, pltpu.SemaphoreType.REGULAR,
+            dma((6,)), dma((4,)), dma((4,)), pltpu.SemaphoreType.REGULAR, pltpu.SemaphoreType.REGULAR,
         ] + sems,
         compiler_params=pltpu.CompilerParams(collective_id=0, has_side_effects=True),
     )(thermal_conductivities, patch_group_label, drain_power_density.reshape(1, clusters),

time: 21.5 us -> 20.7 us (0.963)
  Pallas kernels: 19.4 us -> 18.6 us
    pallas_call x1, Pallas kernels: 19.4 us -> 18.6 us  [per_device(): pl.pallas_call(functools.partial(kernel, sizes, clusters), out_shape=[plt...]
where the time goes in v3:
time: 20.7 us; the launch traced here: 20.5 us
  Pallas kernels  18.6 us (90%)
  local copies, waits for them, and re-layouts  1.26 us (6%)
  between operations  0.64 us (3%)
    pallas_call x1, Pallas kernels, per_device(): pl.pallas_call(functools.partial(kernel, sizes, clusters), out_shape=[plt...  18.6 us
    unnamed x2, local copies, waits for them, and re-layouts  1.26 us

profile of v3, /device:TPU:0, one launch (start us, length us, event | category | flops | bytes accessed | tf_op | source)
XLA Modules:
  0.0 20.5 jit_solution(15834589318975458164)
XLA Ops:
  0.6 18.6 %shard_map.77 = (f32[128,128]{1,0:T(8,128)S(1)}, f32[128,128]{1,0:T(8,128)S(1)}) custom-call(f32[8]{0:T(128)} %cond_hbm.1, s32[1,2,4]{2,1,0:T(2,128)} %label_hbm.1, f32[1,64]{1,0:T(1,128)} %bitcast.11, f32[128,128]{1,0:T(8,128)} %bitcast.8, f32[128,128]{1,0:T(8,128)} %bitcast.9, s32[128,128]{1,0:T(8,128)} %bitcast.10), custom_call_target="tpu_custom_call" | custom-call | tf_op jit(solution)/shard_map/pallas_call | solution.py:429
  19.3 0.6 %copy.10 = f32[8,16,128]{2,1,0:T(8,128)} copy(f32[8,16,128]{2,1,0:T(8,128)S(1)} %bitcast.7) | data formatting | bytes 131072
  19.9 0.6 %copy.11 = f32[8,16,128]{2,1,0:T(8,128)} copy(f32[8,16,128]{2,1,0:T(8,128)S(1)} %bitcast.6) | data formatting | bytes 131072

commit v4 on v3

--- a/solution.py
+++ b/solution.py
@@ -164,10 +164,12 @@
             self.n, self.here = place(axes)
 
         def copies(self, d, slot):
+            step = jnp.where(2 * self.here < self.n, self.n - d, d)
+
             def make(ref):
                 return pltpu.make_async_remote_copy(
                     src_ref=ref, dst_ref=ref, send_sem=self.ssem.at[d - 1], recv_sem=self.rsem.at[slot],
-                    device_id=target(self.axes, lax.rem(self.here + d, self.n)), device_id_type=MESH)
+                    device_id=target(self.axes, lax.rem(self.here + step, self.n)), device_id_type=MESH)
             if self.edge is None:
                 return [(None, make(self.buf.at[slot]))]
             rows, offset = self.edge

time: 20.7 us -> 20.7 us (level)
  no operation moved by 1% of the time
where the time goes in v4:
time: 20.7 us; the launch traced here: 20.6 us
  Pallas kernels  18.6 us (90%)
  local copies, waits for them, and re-layouts  1.26 us (6%)
  between operations  0.64 us (3%)
    pallas_call x1, Pallas kernels, per_device(): pl.pallas_call(functools.partial(kernel, sizes, clusters), out_shape=[plt...  18.6 us
    unnamed x2, local copies, waits for them, and re-layouts  1.26 us

profile of v4, /device:TPU:0, one launch (start us, length us, event | category | flops | bytes accessed | tf_op | source)
XLA Modules:
  0.0 20.6 jit_solution(5240997146934228190)
XLA Ops:
  0.6 18.6 %shard_map.77 = (f32[128,128]{1,0:T(8,128)S(1)}, f32[128,128]{1,0:T(8,128)S(1)}) custom-call(f32[8]{0:T(128)} %cond_hbm.1, s32[1,2,4]{2,1,0:T(2,128)} %label_hbm.1, f32[1,64]{1,0:T(1,128)} %bitcast.11, f32[128,128]{1,0:T(8,128)} %bitcast.8, f32[128,128]{1,0:T(8,128)} %bitcast.9, s32[128,128]{1,0:T(8,128)} %bitcast.10), custom_call_target="tpu_custom_call" | custom-call | tf_op jit(solution)/shard_map/pallas_call | solution.py:431
  19.3 0.6 %copy.10 = f32[8,16,128]{2,1,0:T(8,128)} copy(f32[8,16,128]{2,1,0:T(8,128)S(1)} %bitcast.7) | data formatting | bytes 131072
  19.9 0.6 %copy.11 = f32[8,16,128]{2,1,0:T(8,128)} copy(f32[8,16,128]{2,1,0:T(8,128)S(1)} %bitcast.6) | data formatting | bytes 131072
